TPU v7x, 32 devices: a whole 2x2x4 slice. The times are simulated.
32 devices in a mesh: dp: 8 (over z, y), mp: 4 (over x, core).
Axes of the slice: x: 2, y: 2, z: 4, core: 2. Of those that a mesh axis runs over, the one named last changes fastest.
Arguments:
- tokens: bfloat16 [8192, 2048], P('dp'), may hold values from -6 to 6
- out_cot: bfloat16 [8192, 2048], P('dp'), may hold values from -23 to 23
- lengths: int32 [8], P('dp'), may hold values from 1 to 1024, 6144 in all
- seq_family: int32 [8, 1], P('dp'), may hold values from 0 to 3
- family_tokens: int32 [4], replicated, may hold values from 100000 to 3999999
- norm_master: float32 [2048, 6], P('dp'), may hold values from -0.5 to 2.4, as said below
- attn_bias_master: float32 [2, 2048], P(None, 'mp'), may hold values from -2 to 2
- qkv_master: float32 [2048, 3, 2048], P('dp', None, 'mp'), may hold values from -0.125 to 0.125
- proj_master: float32 [2048, 2048], P('dp', 'mp'), may hold values from -1.5 to 1.5
- fc_bias_master: float32 [8192], P('mp'), may hold values from -1.5 to 1.5
- fc_master: float32 [2048, 8192], P('dp', 'mp'), may hold values from -0.125 to 0.125
- down_master: float32 [2048, 8192], P('dp', 'mp'), may hold values from -0.0625 to 0.0625
- norm_moment: float32 [2048, 6], P('dp'), may hold values from -0.0008544922 to 0.0008544922
- attn_bias_moment: float32 [2, 2048], P(None, 'mp'), may hold values from -0.0008544922 to 0.0008544922
- qkv_moment: float32 [2048, 3, 2048], P('dp', None, 'mp'), may hold values from -0.0008544922 to 0.0008544922
- proj_moment: float32 [2048, 2048], P('dp', 'mp'), may hold values from -0.0008544922 to 0.0008544922
- fc_bias_moment: float32 [8192], P('mp'), may hold values from -0.0008544922 to 0.0008544922
- fc_moment: float32 [2048, 8192], P('dp', 'mp'), may hold values from -0.0008544922 to 0.0008544922
- down_moment: float32 [2048, 8192], P('dp', 'mp'), may hold values from -0.0008544922 to 0.0008544922
- norm_average: float32 [2048, 6], P('dp'), may hold values from 0.5 to 1.5
- attn_bias_average: float32 [2, 2048], P(None, 'mp'), may hold values from -2 to 2
- qkv_average: float32 [2048, 3, 2048], P('dp', None, 'mp'), may hold values from -0.125 to 0.125
- proj_average: float32 [2048, 2048], P('dp', 'mp'), may hold values from -1.5 to 1.5
- fc_bias_average: float32 [8192], P('mp'), may hold values from -1.5 to 1.5
- fc_average: float32 [2048, 8192], P('dp', 'mp'), may hold values from -0.125 to 0.125
- down_average: float32 [2048, 8192], P('dp', 'mp'), may hold values from -0.0625 to 0.0625
Outputs:
- block_out: bfloat16 [8192, 2048], P('dp')
- input_grad: float32 [8192, 2048], P('dp')
- norm_grad: float32 [2048, 6], P('dp')
- attn_bias_grad: float32 [2, 2048], P(None, 'mp')
- qkv_grad: float32 [2048, 3, 2048], P('dp', None, 'mp')
- proj_grad: float32 [2048, 2048], P('dp', 'mp')
- fc_bias_grad: float32 [8192], P('mp')
- fc_grad: float32 [2048, 8192], P('dp', 'mp')
- down_grad: float32 [2048, 8192], P('dp', 'mp')
- norm_momentum: float32 [2048, 6], P('dp')
- attn_bias_momentum: float32 [2, 2048], P(None, 'mp')
- qkv_momentum: float32 [2048, 3, 2048], P('dp', None, 'mp')
- proj_momentum: float32 [2048, 2048], P('dp', 'mp')
- fc_bias_momentum: float32 [8192], P('mp')
- fc_momentum: float32 [2048, 8192], P('dp', 'mp')
- down_momentum: float32 [2048, 8192], P('dp', 'mp')
- norm_averaged: float32 [2048, 6], P('dp')
- attn_bias_averaged: float32 [2, 2048], P(None, 'mp')
- qkv_averaged: float32 [2048, 3, 2048], P('dp', None, 'mp')
- proj_averaged: float32 [2048, 2048], P('dp', 'mp')
- fc_bias_averaged: float32 [8192], P('mp')
- fc_averaged: float32 [2048, 8192], P('dp', 'mp')
- down_averaged: float32 [2048, 8192], P('dp', 'mp')
- norm_updated: float32 [2048, 6], P('dp')
- attn_bias_updated: float32 [2, 2048], P(None, 'mp')
- qkv_updated: float32 [2048, 3, 2048], P('dp', None, 'mp')
- proj_updated: float32 [2048, 2048], P('dp', 'mp')
- fc_bias_updated: float32 [8192], P('mp')
- fc_updated: float32 [2048, 8192], P('dp', 'mp')
- down_updated: float32 [2048, 8192], P('dp', 'mp')
- norm_copy: bfloat16 [2048, 6], P('dp')
- attn_bias_copy: bfloat16 [2, 2048], P(None, 'mp')
- qkv_copy: bfloat16 [2048, 3, 2048], P('dp', None, 'mp')
- proj_copy: bfloat16 [2048, 2048], P('dp', 'mp')
- fc_bias_copy: bfloat16 [8192], P('mp')
- fc_copy: bfloat16 [2048, 8192], P('dp', 'mp')
- down_copy: bfloat16 [2048, 8192], P('dp', 'mp')
- grad_norm: float32 [], replicated
Inputs may be any that keep to these rules, and one draw needn't show every extreme that they name: `lengths`: they sum to 6144; the longest is 1024. `seq_family`: every family has a sequence. `norm_master`: gains positive, biases of either sign.
All inputs are finite; a program needn't handle non-finite values. No bound on the sum of `lengths` on one device may be relied on, other than what follows from the above.
Results may differ from a plain program's by a relative error of at most 0.012.
The roundings to bfloat16 on the way count: a program that leaves them out, or rounds other values in their place, can miss the bound.
Values may be sent and summed in bfloat16 or wider, within the bound.
A program may use at most 256 MiB of HBM per device.

v0:
```python
import math
import jax
import jax.numpy as jnp
from jax import lax
from jax.sharding import PartitionSpec as P

HEAD_DIM = 128
LEN = 1024
EPS = 1e-05
MOMENTUM = 0.9
RATE = 192.0
KEEP = 0.9
NEG = -1e30


def layer_norm(value, gain, shift):
    centre = jnp.mean(value, axis=-1, keepdims=True)
    centred = value - centre
    spread = jnp.mean(centred * centred, axis=-1, keepdims=True)
    return centred * lax.rsqrt(spread + EPS) * gain + shift


def gelu_tanh(value):
    return (
        0.5
        * value
        * (1.0 + jnp.tanh(0.7978845608028654 * (value + 0.044715 * value * value * value)))
    )


def local(
    tokens,
    out_cot,
    lengths,
    seq_family,
    family_tokens,
    norm_master,
    attn_bias_master,
    qkv_master,
    proj_master,
    fc_bias_master,
    fc_master,
    down_master,
    norm_moment,
    attn_bias_moment,
    qkv_moment,
    proj_moment,
    fc_bias_moment,
    fc_moment,
    down_moment,
    norm_average,
    attn_bias_average,
    qkv_average,
    proj_average,
    fc_bias_average,
    fc_average,
    down_average,
):
    seq_count = lengths.shape[0]
    row_count = tokens.shape[0]
    seq_len = row_count // seq_count
    family_count = family_tokens.shape[0]
    local_heads = qkv_master.shape[2] // HEAD_DIM
    head_width = qkv_master.shape[2]
    scale = 1.0 / math.sqrt(HEAD_DIM)
    mp_count = lax.axis_size("mp")
    dp_count = lax.axis_size("dp")

    def sum_over_mp(term_fn):
        summed = lax.psum(term_fn(0, row_count), "mp")
        return summed

    family_ids = jnp.arange(family_count, dtype=jnp.int32)
    member = seq_family == family_ids[None, :]
    local_counts = jnp.sum(jnp.where(member, lengths[:, None], 0), axis=0).astype(jnp.float32)
    counts = lax.psum(local_counts, "dp")
    valid_total = jnp.sum(counts)
    share = family_tokens.astype(jnp.float32) / jnp.sum(family_tokens).astype(jnp.float32)
    family_weight = share * valid_total / jnp.maximum(counts, float(LEN // 2))
    seq_weight = jnp.sum(jnp.where(member, family_weight[None, :], 0.0), axis=1)
    places = jnp.arange(seq_len, dtype=jnp.int32)
    token_weight = jnp.where(places[None, :] < lengths[:, None], seq_weight[:, None], 0.0).reshape(
        row_count
    )
    causal = places[:, None] >= places[None, :]
    low_norm = norm_master.astype(jnp.bfloat16)
    low_qkv = qkv_master.astype(jnp.bfloat16)
    low_proj = proj_master.astype(jnp.bfloat16)
    low_fc = fc_master.astype(jnp.bfloat16)
    low_down = down_master.astype(jnp.bfloat16)
    w_qkv, w_proj, w_fc, w_down, w_norm = (
        lax.all_gather(low_qkv, "dp", axis=0, tiled=True),
        lax.all_gather(low_proj, "dp", axis=0, tiled=True),
        lax.all_gather(low_fc, "dp", axis=0, tiled=True),
        lax.all_gather(low_down, "dp", axis=0, tiled=True),
        lax.all_gather(low_norm, "dp", axis=0, tiled=True),
    )
    norm_full = w_norm.astype(jnp.float32)
    bias_rows = jnp.stack(
        [attn_bias_master[0], jnp.zeros_like(attn_bias_master[0]), attn_bias_master[1]], axis=0
    )
    x_in = tokens.astype(jnp.float32)
    ln1_low = layer_norm(x_in, norm_full[:, 0], norm_full[:, 1]).astype(jnp.bfloat16)
    qkv = (
        jnp.einsum("td,dce->tce", ln1_low, w_qkv, preferred_element_type=jnp.float32)
        + bias_rows[None]
    )
    qkv = qkv.astype(jnp.bfloat16)
    heads = qkv.reshape(seq_count, seq_len, 3, local_heads, HEAD_DIM)

    def attend(one_seq):
        query_rows = one_seq[:, 0]
        key_rows = one_seq[:, 1]
        value_rows = one_seq[:, 2]
        scores = (
            jnp.einsum("qhd,khd->hqk", query_rows, key_rows, preferred_element_type=jnp.float32)
            * scale
        )
        scores = jnp.where(causal[None], scores, NEG)
        row_top = jnp.max(scores, axis=-1, keepdims=True)
        log_total = row_top + jnp.log(jnp.sum(jnp.exp(scores - row_top), axis=-1, keepdims=True))
        attn_prob = jnp.exp(scores - log_total).astype(jnp.bfloat16)
        mixed = jnp.einsum(
            "hqk,khd->qhd", attn_prob, value_rows, preferred_element_type=jnp.float32
        )
        return (mixed.astype(jnp.bfloat16), log_total)

    mixed_low, log_kept = lax.map(attend, heads)
    mixed_low = mixed_low.reshape(row_count, head_width)

    def attn_term(start, count):
        return jnp.einsum("te,de->td", mixed_low, w_proj, preferred_element_type=jnp.float32)

    residual_part = x_in + sum_over_mp(attn_term) + norm_full[:, 4]
    ln2_part, ln2_back = jax.vjp(layer_norm, residual_part, norm_full[:, 2], norm_full[:, 3])
    ln2_low = ln2_part.astype(jnp.bfloat16)
    pre_act = (
        jnp.einsum("td,df->tf", ln2_low, w_fc, preferred_element_type=jnp.float32)
        + fc_bias_master[None]
    )
    hidden_act, gelu_back = jax.vjp(gelu_tanh, pre_act)
    hidden_low = hidden_act.astype(jnp.bfloat16)

    def mlp_term(start, count):
        return jnp.einsum("tf,df->td", hidden_low, w_down, preferred_element_type=jnp.float32)

    block_part = (residual_part + sum_over_mp(mlp_term) + norm_full[:, 5]).astype(jnp.bfloat16)
    upstream = token_weight[:, None] * out_cot.astype(jnp.float32)
    upstream_low = upstream.astype(jnp.bfloat16)
    down_sum = jnp.einsum("td,tf->df", upstream_low, hidden_low, preferred_element_type=jnp.float32)
    back_act = jnp.einsum("td,df->tf", upstream_low, w_down, preferred_element_type=jnp.float32)
    back_pre = gelu_back(back_act)[0].astype(jnp.bfloat16)
    fc_bias_sum = jnp.sum(back_pre, axis=0, dtype=jnp.float32)
    fc_sum = jnp.einsum("td,tf->df", ln2_low, back_pre, preferred_element_type=jnp.float32)

    def fc_back_term(start, count):
        return jnp.einsum("tf,df->td", back_pre, w_fc, preferred_element_type=jnp.float32)

    back_ln2 = sum_over_mp(fc_back_term)
    back_resid_part, gain2_sum, shift2_sum = ln2_back(back_ln2)
    back_resid_part = upstream + back_resid_part
    back_attn_low = back_resid_part.astype(jnp.bfloat16)
    proj_sum = jnp.einsum("td,te->de", back_attn_low, mixed_low, preferred_element_type=jnp.float32)
    back_mixed = jnp.einsum(
        "td,de->te", back_attn_low, w_proj, preferred_element_type=jnp.float32
    ).astype(jnp.bfloat16)
    back_mixed = back_mixed.reshape(seq_count, seq_len, local_heads, HEAD_DIM)

    def attend_back(items):
        one_seq, log_total, back_seq = items
        query_rows = one_seq[:, 0]
        key_rows = one_seq[:, 1]
        value_rows = one_seq[:, 2]
        scores = (
            jnp.einsum("qhd,khd->hqk", query_rows, key_rows, preferred_element_type=jnp.float32)
            * scale
        )
        scores = jnp.where(causal[None], scores, NEG)
        attn_prob = jnp.exp(scores - log_total)
        prob_low = attn_prob.astype(jnp.bfloat16)
        back_value = jnp.einsum(
            "hqk,qhd->khd", prob_low, back_seq, preferred_element_type=jnp.float32
        )
        back_prob = jnp.einsum(
            "qhd,khd->hqk", back_seq, value_rows, preferred_element_type=jnp.float32
        )
        back_score = attn_prob * (
            back_prob - jnp.sum(attn_prob * back_prob, axis=-1, keepdims=True)
        )
        back_score = back_score.astype(jnp.bfloat16)
        back_query = (
            jnp.einsum("hqk,khd->qhd", back_score, key_rows, preferred_element_type=jnp.float32)
            * scale
        )
        back_key = (
            jnp.einsum("hqk,qhd->khd", back_score, query_rows, preferred_element_type=jnp.float32)
            * scale
        )
        return jnp.stack([back_query, back_key, back_value], axis=1).astype(jnp.bfloat16)

    back_heads = lax.map(attend_back, (heads, log_kept, back_mixed))
    back_qkv = back_heads.reshape(row_count, 3, head_width)
    attn_bias_sum = jnp.sum(back_qkv[:, 0::2], axis=0, dtype=jnp.float32)
    qkv_sum = jnp.einsum("td,tce->dce", ln1_low, back_qkv, preferred_element_type=jnp.float32)

    def qkv_back_term(start, count):
        return jnp.einsum("tce,dce->td", back_qkv, w_qkv, preferred_element_type=jnp.float32)

    back_ln1 = sum_over_mp(qkv_back_term)
    ln1_again, ln1_back = jax.vjp(layer_norm, x_in, norm_full[:, 0], norm_full[:, 1])
    back_input, gain1_sum, shift1_sum = ln1_back(back_ln1)
    whole = back_resid_part + back_input
    norm_part = jnp.stack(
        [
            gain1_sum,
            shift1_sum,
            gain2_sum,
            shift2_sum,
            jnp.sum(back_resid_part, axis=0),
            jnp.sum(upstream, axis=0),
        ],
        axis=1,
    )
    qkv_reduced, proj_reduced, fc_reduced, down_reduced, norm_reduced = (
        lax.psum_scatter(qkv_sum, "dp", scatter_dimension=0, tiled=True),
        lax.psum_scatter(proj_sum, "dp", scatter_dimension=0, tiled=True),
        lax.psum_scatter(fc_sum, "dp", scatter_dimension=0, tiled=True),
        lax.psum_scatter(down_sum, "dp", scatter_dimension=0, tiled=True),
        lax.psum_scatter(norm_part, "dp", scatter_dimension=0, tiled=True),
    )
    attn_bias_reduced, fc_bias_reduced = lax.psum((attn_bias_sum, fc_bias_sum), "dp")
    raw_grads = [
        reduced / valid_total
        for reduced in (
            norm_reduced,
            attn_bias_reduced,
            qkv_reduced,
            proj_reduced,
            fc_bias_reduced,
            fc_reduced,
            down_reduced,
        )
    ]
    local_squares = jnp.sum(raw_grads[0] * raw_grads[0]) / float(mp_count)
    local_squares = local_squares + jnp.sum(raw_grads[1] * raw_grads[1]) / float(dp_count)
    local_squares = local_squares + jnp.sum(raw_grads[4] * raw_grads[4]) / float(dp_count)
    for grad_raw in (raw_grads[2], raw_grads[3], raw_grads[5], raw_grads[6]):
        local_squares = local_squares + jnp.sum(grad_raw * grad_raw)
    squares = lax.psum(local_squares, ("dp", "mp"))
    grad_norm = jnp.sqrt(squares)
    clip_factor = jnp.minimum(1.0, 1.0 / (grad_norm + 1e-06))
    masters = (
        norm_master,
        attn_bias_master,
        qkv_master,
        proj_master,
        fc_bias_master,
        fc_master,
        down_master,
    )
    moments = (
        norm_moment,
        attn_bias_moment,
        qkv_moment,
        proj_moment,
        fc_bias_moment,
        fc_moment,
        down_moment,
    )
    averages = (
        norm_average,
        attn_bias_average,
        qkv_average,
        proj_average,
        fc_bias_average,
        fc_average,
        down_average,
    )
    grads_out = []
    momenta_out = []
    averaged_out = []
    updated_out = []
    copies_out = []
    for master, moment, average, grad_raw in zip(masters, moments, averages, raw_grads):
        clipped = grad_raw * clip_factor
        momentum = MOMENTUM * moment + clipped
        updated = master - RATE * (clipped + MOMENTUM * momentum)
        averaged = KEEP * average + (1.0 - KEEP) * updated
        grads_out.append(clipped)
        momenta_out.append(momentum)
        averaged_out.append(averaged)
        updated_out.append(updated)
        copies_out.append(updated.astype(jnp.bfloat16))
    return (
        block_part,
        whole,
        grads_out[0],
        grads_out[1],
        grads_out[2],
        grads_out[3],
        grads_out[4],
        grads_out[5],
        grads_out[6],
        momenta_out[0],
        momenta_out[1],
        momenta_out[2],
        momenta_out[3],
        momenta_out[4],
        momenta_out[5],
        momenta_out[6],
        averaged_out[0],
        averaged_out[1],
        averaged_out[2],
        averaged_out[3],
        averaged_out[4],
        averaged_out[5],
        averaged_out[6],
        updated_out[0],
        updated_out[1],
        updated_out[2],
        updated_out[3],
        updated_out[4],
        updated_out[5],
        updated_out[6],
        copies_out[0],
        copies_out[1],
        copies_out[2],
        copies_out[3],
        copies_out[4],
        copies_out[5],
        copies_out[6],
        grad_norm,
    )


def solution(mesh):
    placed = (
        P("dp", None),
        P("dp", None),
        P("dp"),
        P("dp", None),
        P(),
        P("dp", None),
        P(None, "mp"),
        P("dp", None, "mp"),
        P("dp", "mp"),
        P("mp"),
        P("dp", "mp"),
        P("dp", "mp"),
        P("dp", None),
        P(None, "mp"),
        P("dp", None, "mp"),
        P("dp", "mp"),
        P("mp"),
        P("dp", "mp"),
        P("dp", "mp"),
        P("dp", None),
        P(None, "mp"),
        P("dp", None, "mp"),
        P("dp", "mp"),
        P("mp"),
        P("dp", "mp"),
        P("dp", "mp"),
    )
    return jax.shard_map(
        local,
        mesh=mesh,
        in_specs=placed,
        out_specs=(
            P("dp", None),
            P("dp", None),
            P("dp", None),
            P(None, "mp"),
            P("dp", None, "mp"),
            P("dp", "mp"),
            P("mp"),
            P("dp", "mp"),
            P("dp", "mp"),
            P("dp", None),
            P(None, "mp"),
            P("dp", None, "mp"),
            P("dp", "mp"),
            P("mp"),
            P("dp", "mp"),
            P("dp", "mp"),
            P("dp", None),
            P(None, "mp"),
            P("dp", None, "mp"),
            P("dp", "mp"),
            P("mp"),
            P("dp", "mp"),
            P("dp", "mp"),
            P("dp", None),
            P(None, "mp"),
            P("dp", None, "mp"),
            P("dp", "mp"),
            P("mp"),
            P("dp", "mp"),
            P("dp", "mp"),
            P("dp", None),
            P(None, "mp"),
            P("dp", None, "mp"),
            P("dp", "mp"),
            P("mp"),
            P("dp", "mp"),
            P("dp", "mp"),
            P(),
        ),
        check_vma=False,
    )
```

profile of v0, /device:TPU:0, one launch (start us, length us, event | category | flops | bytes accessed | tf_op | source)
XLA Modules:
  0.0 2152.3 jit_solution(12280135592228971859)
XLA Ops:
  7.3 2.6 copy.64
  9.9 1.8 convert_element_type.116
  12.8 2.8 convert_reduce_fusion
  15.6 3.4 fusion.15
  19.1 32.9 %all_gather.15 = bf16[2048,6]{0,1:T(8,128)(2,1)S(1)} all-gather(bf16[256,6]{0,1:T(8,128)(2,1)S(1)} %convert_element_type.108), channel_id=1, replica_groups=mesh['dp'=8,'mp'=4] {'dp'}, dimensions={0}, use_global_device_ids=true | all-gather | bytes 27648 | tf_op jit(solution)/shard_map/all_gather | solution.py:96
  52.7 61.0 %all-gather.5.cloned.1.call-done = bf16[2048,3,512]{0,2,1:T(8,128)(2,1)} async-done(((bf16[256,3,512]{0,2,1:T(8,128)(2,1)}), bf16[2048,3,512]{0,2,1:T(8,128)(2,1)}) %all-gather.5.cloned.1.call-update) | async-done | bytes 6291472 | tf_op jit(solution)/shard_map/all_gather | solution.py:92
  113.7 11.1 add_convert_fusion.2
  124.9 3.3 fusion
  128.3 3.7 exponential_reduce_fusion
  132.0 2.0 copy-done.2
  134.0 6.5 convolution_convert_fusion.1
  140.5 23.5 %all-gather.7.cloned.1.call-done = bf16[2048,512]{1,0:T(8,128)(2,1)} async-done(((bf16[256,512]{1,0:T(8,128)(2,1)}), bf16[2048,512]{1,0:T(8,128)(2,1)}) %all-gather.7.cloned.1.call-update) | async-done | bytes 2097168 | tf_op jit(solution)/shard_map/all_gather | solution.py:93
  164.0 7.4 fusion.66
  171.5 2.7 convert_element_type.118
  174.3 3.2 convert_element_type.120
  178.8 18.5 psum.58
  201.1 121.8 %all-reduce.6.cloned.1.call-done = f32[1024,2048]{1,0:T(8,128)} async-done(((f32[1024,2048]{1,0:T(8,128)}), f32[1024,2048]{1,0:T(8,128)}) %all-reduce.6.cloned.1.call-update) | async-done | bytes 8388624 | tf_op jit(solution)/shard_map/psum | solution.py:70
  322.9 5.8 fusion.62
  328.7 3.3 copy-done
  333.0 117.6 %all-gather.9.cloned.1.call-done = bf16[2048,2048]{1,0:T(8,128)(2,1)} async-done(((bf16[256,2048]{1,0:T(8,128)(2,1)}), bf16[2048,2048]{1,0:T(8,128)(2,1)}) %all-gather.9.cloned.1.call-update) | async-done | bytes 8388624 | tf_op jit(solution)/shard_map/all_gather | solution.py:94
  450.6 15.9 fusion.51
  466.5 109.8 %all-gather.11.cloned.1.call-done = bf16[2048,2048]{1,0:T(8,128)(2,1)} async-done(((bf16[256,2048]{1,0:T(8,128)(2,1)}), bf16[2048,2048]{1,0:T(8,128)(2,1)}) %all-gather.11.cloned.1.call-update) | async-done | bytes 8388624 | tf_op jit(solution)/shard_map/all_gather | solution.py:95
  576.3 21.0 convert_reduce_fusion.1
  597.3 1.9 copy-done.58
  599.2 11.1 fusion.67
  610.3 18.3 fusion.49
  628.6 132.9 %all-reduce.8.cloned.1.call-done = f32[1024,2048]{1,0:T(8,128)} async-done(((f32[1024,2048]{1,0:T(8,128)}), f32[1024,2048]{1,0:T(8,128)}) %all-reduce.8.cloned.1.call-update) | async-done | bytes 8388624 | tf_op jit(solution)/shard_map/psum | solution.py:70
  761.5 7.5 multiply_reduce_fusion.1
  769.7 5.0 fusion.61
  774.7 6.3 fusion.33
  781.1 9.7 convolution_convert_fusion
  790.7 12.6 multiply_reduce_fusion
  803.3 12.1 multiply_convert_fusion
  815.5 2.9 multiply_convert_fusion.2
  819.7 1.5 copy.77
  823.1 11.0 convolution_bitcast_fusion
  835.3 9.5 fusion.23
  844.9 278.3 %all-reduce.10.cloned.1.call-done = (f32[1024,2048]{1,0:T(8,128)}, f32[1024,2048]{1,0:T(8,128)}) async-done(((f32[1024,2048]{1,0:T(8,128)}, f32[1024,2048]{1,0:T(8,128)}), (f32[1024,2048]{1,0:T(8,128)}, f32[1024,2048]{1,0:T(8,128)})) %all-reduce.10.cloned.1.call-update) | async-done | bytes 16777232 | tf_op jit(solution)/shard_map/psum | solution.py:70
  1123.3 6.4 fusion.53
  1129.7 1.9 copy-done.3
  1131.6 3.9 fusion.10
  1135.5 10.2 fusion.20
  1146.7 13.6 fusion.36
  1161.0 16.4 fusion.50
  1177.7 17.1 fusion.27
  1195.5 37.8 %all-reduce = (f32[2,512]{1,0:T(2,128)S(1)}, f32[2048]{0:T(1024)S(1)}) all-reduce(f32[2,512]{1,0:T(2,128)S(1)} %convert_reduce_fusion.2, f32[2048]{0:T(1024)S(1)} %copy-done.48), channel_id=1, replica_groups=mesh['dp'=8,'mp'=4] {'dp'}, use_global_device_ids=true, to_apply=%region_28.29 | all-reduce | flops 3072 | bytes 24576 | tf_op jit(solution)/shard_map/psum | solution.py:231
  1237.2 2.4 multiply_reduce_fusion.7
  1239.6 41.7 %reduce-scatter.6.cloned.1.call-done = f32[256,6]{0,1:T(8,128)} async-done(((f32[2048,6]{0,1:T(8,128)}), f32[256,6]{0,1:T(8,128)}) %reduce-scatter.6.cloned.1.call-update) | async-done | bytes 6160 | tf_op jit(solution)/shard_map/reduce_scatter | solution.py:229
  1281.2 2.0 multiply_reduce_fusion.9
  1283.9 208.1 %reduce-scatter.8.cloned.1.call-done = f32[256,3,512]{2,0,1:T(8,128)} async-done(((f32[2048,3,512]{2,0,1:T(8,128)}), f32[256,3,512]{2,0,1:T(8,128)}) %reduce-scatter.8.cloned.1.call-update) | async-done | bytes 1572880 | tf_op jit(solution)/shard_map/reduce_scatter | solution.py:225
  1492.0 3.1 multiply_reduce_fusion.6
  1496.3 280.9 %reduce-scatter.12.cloned.1.call-done = f32[256,2048]{1,0:T(8,128)} async-done(((f32[2048,2048]{1,0:T(8,128)}), f32[256,2048]{1,0:T(8,128)}) %reduce-scatter.12.cloned.1.call-update) | async-done | bytes 2097168 | tf_op jit(solution)/shard_map/reduce_scatter | solution.py:227
  1777.2 3.4 multiply_reduce_fusion.5
  1781.3 281.4 %reduce-scatter.14.cloned.1.call-done = f32[256,2048]{1,0:T(8,128)} async-done(((f32[2048,2048]{1,0:T(8,128)}), f32[256,2048]{1,0:T(8,128)}) %reduce-scatter.14.cloned.1.call-update) | async-done | bytes 2097168 | tf_op jit(solution)/shard_map/reduce_scatter | solution.py:228
  2062.7 3.4 multiply_reduce_fusion.4
  2066.9 10.2 add_convert_fusion
  2077.0 39.2 %psum.63 = f32[]{:T(128)} all-reduce(f32[]{:T(128)S(6)} %add.249), channel_id=1, replica_groups=mesh['dp'=8,'mp'=4] {'dp','mp'}, use_global_device_ids=true, to_apply=%region_41.42 | all-reduce | flops 1 | bytes 8 | tf_op jit(solution)/shard_map/psum | solution.py:249
  2122.0 3.2 fusion.57
  2125.3 2.2 multiply_add_fusion.8
  2127.5 5.9 fusion.58
  2133.4 1.7 multiply_add_fusion.6
  2135.1 5.1 fusion.54
  2140.3 2.0 multiply_add_fusion.2
  2142.3 1.7 multiply_add_fusion.3
  (174 shorter events, 22.0 us)
Async XLA Ops:
  7.2 11.8 copy-start.40
  7.2 106.5 %all-gather.5.cloned.1.call-start = ((), (), s32[]{:S(2)}) async-start(), calls=%async_computation.5 | async-start | bytes 7077888 | tf_op jit(solution)/shard_map/all_gather | solution.py:92
  9.9 154.1 %all-gather.7.cloned.1.call-start = ((), (), s32[]{:S(2)}) async-start(), calls=%async_computation.6 | async-start | bytes 2359296 | tf_op jit(solution)/shard_map/all_gather | solution.py:93
  11.7 311.2 %all-reduce.6.cloned.1.call-start = ((), (), s32[]{:S(2)}) async-start(), calls=%async_computation.7 | async-start | bytes 16777216 | tf_op jit(solution)/shard_map/psum | solution.py:70
  15.6 109.2 %copy-start.28 = (f32[1024]{0:T(1024)}, f32[1024]{0:T(1024)S(1)}, u32[]{:S(2)}) copy-start(f32[1024]{0:T(1024)S(1)} %broadcast_multiply_fusion.8) | copy-start | bytes 12292
  19.0 105.8 %copy-start.32 = (f32[1024]{0:T(1024)}, f32[1024]{0:T(1024)S(1)}, u32[]{:S(2)}) copy-start(f32[1024]{0:T(1024)S(1)} %fusion.15) | copy-start | bytes 12292
  19.1 105.8 %copy-start.30 = (f32[1024]{0:T(1024)}, f32[1024]{0:T(1024)S(1)}, u32[]{:S(2)}) copy-start(f32[1024]{0:T(1024)S(1)} %fusion.42) | copy-start | bytes 12292
  52.6 72.3 %copy-start.26 = (f32[2048,1]{0,1:T(1,128)}, f32[2048,1]{0,1:T(1,128)S(1)}, u32[]{:S(2)}) copy-start(f32[2048,1]{0,1:T(1,128)S(1)} %get-tuple-element.123) | copy-start | bytes 24580
  52.6 72.3 %copy-start.46 = (f32[2048,1]{0,1:T(1,128)}, f32[2048,1]{0,1:T(1,128)S(1)}, u32[]{:S(2)}) copy-start(f32[2048,1]{0,1:T(1,128)S(1)} %get-tuple-element.124) | copy-start | bytes 24580
  52.6 398.0 %copy-start.44 = (f32[2048,1]{0,1:T(1,128)}, f32[2048,1]{0,1:T(1,128)S(1)}, u32[]{:S(2)}) copy-start(f32[2048,1]{0,1:T(1,128)S(1)} %get-tuple-element.121) | copy-start | bytes 24580
  128.3 5.7 copy-start.2
  140.4 31.0 %copy-start.56 = (bf16[4,128,1024]{2,1,0:T(8,128)(2,1)}, bf16[4,128,1024]{2,1,0:T(8,128)(2,1)S(1)}, u32[]{:S(2)}) copy-start(bf16[4,128,1024]{2,1,0:T(8,128)(2,1)S(1)} %convolution_convert_fusion.1) | copy-start | bytes 3145732
  171.4 25.9 %copy-start.54 = (s32[4]{0:T(128)S(1)}, s32[4]{0:T(128)}, u32[]{:S(2)}) copy-start(s32[4]{0:T(128)} %param.30) | copy-start | bytes 52
  171.4 279.2 %all-gather.9.cloned.1.call-start = ((), (), s32[]{:S(2)}) async-start(), calls=%async_computation.8 | async-start | bytes 9437184 | tf_op jit(solution)/shard_map/all_gather | solution.py:94
  174.2 402.1 %all-gather.11.cloned.1.call-start = ((), (), s32[]{:S(2)}) async-start(), calls=%async_computation.9 | async-start | bytes 9437184 | tf_op jit(solution)/shard_map/all_gather | solution.py:95
  177.5 584.0 %all-reduce.8.cloned.1.call-start = ((), (), s32[]{:S(2)}) async-start(), calls=%async_computation.10 | async-start | bytes 16777216 | tf_op jit(solution)/shard_map/psum | solution.py:70
  450.6 125.7 %copy-start.49 = (f32[2048]{0:T(1024)S(1)}, f32[2048]{0:T(1024)}, u32[]{:S(2)}) copy-start(f32[2048]{0:T(1024)} %param.35) | copy-start | bytes 24580
  576.3 22.9 %copy-start.55 = (bf16[2048,2048]{1,0:T(8,128)(2,1)S(1)}, bf16[2048,2048]{1,0:T(8,128)(2,1)}, u32[]{:S(2)}) copy-start(bf16[2048,2048]{1,0:T(8,128)(2,1)} %all-gather.9.cloned.1.call-done) | copy-start | bytes 25165828
  610.3 513.0 %all-reduce.10.cloned.1.call-start = ((), (), s32[]{:S(2)}) async-start(), calls=%async_computation.16 | async-start | bytes 33554432 | tf_op jit(solution)/shard_map/psum | solution.py:70
  761.5 8.2 copy-start.5
  769.7 5.0 copy-start.15
  774.7 6.4 copy-start.4
  781.1 9.7 copy-start.19
  834.1 289.2 %copy-start.27 = (f32[2048,1]{0,1:T(1,128)S(1)}, f32[2048,1]{0,1:T(1,128)}, u32[]{:S(2)}) copy-start(f32[2048,1]{0,1:T(1,128)} %copy-done.26) | copy-start | bytes 24580
  834.1 289.1 %copy-start.29 = (f32[1024]{0:T(1024)S(1)}, f32[1024]{0:T(1024)}, u32[]{:S(2)}) copy-start(f32[1024]{0:T(1024)} %copy-done.28) | copy-start | bytes 12292
  834.1 403.0 %reduce-scatter.10.cloned.1.call-start = ((), (), s32[]{:S(2)}) async-start(), calls=%async_computation.13 | async-start | bytes 4718592 | tf_op jit(solution)/shard_map/reduce_scatter | solution.py:226
  844.8 284.8 %copy-start.33 = (f32[1024]{0:T(1024)S(1)}, f32[1024]{0:T(1024)}, u32[]{:S(2)}) copy-start(f32[1024]{0:T(1024)} %copy-done.32) | copy-start | bytes 12292
  844.8 284.8 %copy-start.31 = (f32[1024]{0:T(1024)S(1)}, f32[1024]{0:T(1024)}, u32[]{:S(2)}) copy-start(f32[1024]{0:T(1024)} %copy-done.30) | copy-start | bytes 12292
  844.9 436.4 %reduce-scatter.6.cloned.1.call-start = ((), (), s32[]{:S(2)}) async-start(), calls=%async_computation.11 | async-start | bytes 73728 | tf_op jit(solution)/shard_map/reduce_scatter | solution.py:229
  1123.3 6.4 copy-start.1
  1123.3 8.3 copy-start.3
  1129.6 5.9 copy-start.16
  1135.5 11.2 copy-start.17
  1135.5 11.2 copy-start.47
  1146.5 345.5 %reduce-scatter.8.cloned.1.call-start = ((), (), s32[]{:S(2)}) async-start(), calls=%async_computation.12 | async-start | bytes 14155776 | tf_op jit(solution)/shard_map/reduce_scatter | solution.py:225
  1160.3 616.9 %reduce-scatter.12.cloned.1.call-start = ((), (), s32[]{:S(2)}) async-start(), calls=%async_computation.14 | async-start | bytes 18874368 | tf_op jit(solution)/shard_map/reduce_scatter | solution.py:227
  1177.4 885.3 %reduce-scatter.14.cloned.1.call-start = ((), (), s32[]{:S(2)}) async-start(), calls=%async_computation.15 | async-start | bytes 18874368 | tf_op jit(solution)/shard_map/reduce_scatter | solution.py:228
  1194.8 871.9 %copy-start.34 = (f32[2048,1]{0,1:T(1,128)S(1)}, f32[2048,1]{0,1:T(1,128)}, u32[]{:S(2)}) copy-start(f32[2048,1]{0,1:T(1,128)} %get-tuple-element.119) | copy-start | bytes 24580
  2066.7 50.2 %copy-start.50 = (f32[2048]{0:T(1024)S(1)}, f32[2048]{0:T(1024)}, u32[]{:S(2)}) copy-start(f32[2048]{0:T(1024)} %param.42) | copy-start | bytes 24580
  2066.8 51.6 %copy-start.41 = (f32[2,512]{1,0:T(2,128)S(1)}, f32[2,512]{1,0:T(2,128)}, u32[]{:S(2)}) copy-start(f32[2,512]{1,0:T(2,128)} %param.32) | copy-start | bytes 12292
  2066.8 51.6 %copy-start.53 = (f32[2,512]{1,0:T(2,128)S(1)}, f32[2,512]{1,0:T(2,128)}, u32[]{:S(2)}) copy-start(f32[2,512]{1,0:T(2,128)} %param.39) | copy-start | bytes 12292
  2066.8 52.2 %copy-start.52 = (f32[2,512]{1,0:T(2,128)S(1)}, f32[2,512]{1,0:T(2,128)}, u32[]{:S(2)}) copy-start(f32[2,512]{1,0:T(2,128)} %param.46) | copy-start | bytes 12292
  2066.8 52.7 %copy-start.42 = (f32[2048]{0:T(1024)S(1)}, f32[2048]{0:T(1024)}, u32[]{:S(2)}) copy-start(f32[2048]{0:T(1024)} %param.49) | copy-start | bytes 24580
  2066.8 53.3 %copy-start.37 = (f32[256,6]{0,1:T(8,128)S(1)}, f32[256,6]{0,1:T(8,128)}, u32[]{:S(2)}) copy-start(f32[256,6]{0,1:T(8,128)} %param.31) | copy-start | bytes 18436
  2066.8 53.3 %copy-start.38 = (f32[256,6]{0,1:T(8,128)S(1)}, f32[256,6]{0,1:T(8,128)}, u32[]{:S(2)}) copy-start(f32[256,6]{0,1:T(8,128)} %reduce-scatter.6.cloned.1.call-done) | copy-start | bytes 18436
  2066.8 53.3 %copy-start.51 = (f32[256,6]{0,1:T(8,128)S(1)}, f32[256,6]{0,1:T(8,128)}, u32[]{:S(2)}) copy-start(f32[256,6]{0,1:T(8,128)} %param.38) | copy-start | bytes 18436
  2066.8 54.6 %copy-start.43 = (f32[256,6]{0,1:T(8,128)S(1)}, f32[256,6]{0,1:T(8,128)}, u32[]{:S(2)}) copy-start(f32[256,6]{0,1:T(8,128)} %param.45) | copy-start | bytes 18436
  2066.9 60.6 %copy-start.12 = (f32[256,3,512]{2,0,1:T(8,128)S(1)}, f32[256,3,512]{2,0,1:T(8,128)}, u32[]{:S(2)}) copy-start(f32[256,3,512]{2,0,1:T(8,128)} %param.33) | copy-start | bytes 4718596
  2066.9 60.6 %copy-start.13 = (f32[256,3,512]{2,0,1:T(8,128)S(1)}, f32[256,3,512]{2,0,1:T(8,128)}, u32[]{:S(2)}) copy-start(f32[256,3,512]{2,0,1:T(8,128)} %reduce-scatter.8.cloned.1.call-done) | copy-start | bytes 4718596
  2116.9 16.5 copy-start.25
  2118.3 16.7 copy-start.35
  2118.9 16.1 copy-start.39
  2121.4 13.7 copy-start.36
  2125.3 15.0 copy-start.22
  2125.3 9.8 copy-start.8
  2125.3 9.8 copy-start.9
  2125.3 9.8 copy-start.10
  2125.3 9.8 copy-start.11
  2125.3 9.8 copy-start.23
  2125.3 9.8 copy-start.24
  2133.4 6.9 copy-start.14
  2135.1 5.2 copy-start.20
  2135.1 7.2 copy-start.21
  2140.3 3.8 copy-start.6
  (7 other events, 15.0 us)
Sparse Core Ops, SparseCore 0:
  10.7 102.9 all-gather.4
  116.4 47.5 all-gather.6
  171.5 151.3 all-reduce.5
  325.5 125.0 all-gather.8
  453.1 123.1 all-gather.10
  610.4 151.0 all-reduce.7
  834.2 288.9 all-reduce.9
  1127.5 88.2 reduce-scatter.9
  1220.1 61.1 reduce-scatter.5
  1285.1 206.7 reduce-scatter.7
  1496.2 280.9 reduce-scatter.11
  1780.9 281.7 reduce-scatter.13
where the time goes:
time: 2160 us; the launch traced here: 2150 us
  waiting for transfers between devices  1660 us (77%)
  matrix products  195 us (9%)
  other arithmetic  128 us (6%)
  blocking collectives  128 us (6%)
  between operations  23.6 us (1%)
    psum x3, waiting for transfers between devices, sum_over_mp(): summed = lax.psum(term_fn(0, row_count), 'mp')  533 us
    reduce_scatter x1, waiting for transfers between devices, local(): lax.psum_scatter(down_sum, 'dp', scatter_dimension=0, tiled=True)  281 us
    reduce_scatter x1, waiting for transfers between devices, local(): lax.psum_scatter(fc_sum, 'dp', scatter_dimension=0, tiled=True)  281 us
    reduce_scatter x1, waiting for transfers between devices, local(): lax.psum_scatter(qkv_sum, 'dp', scatter_dimension=0, tiled=True)  208 us
    all_gather x1, waiting for transfers between devices, local(): lax.all_gather(low_fc, 'dp', axis=0, tiled=True)  118 us
    all_gather x1, waiting for transfers between devices, local(): lax.all_gather(low_down, 'dp', axis=0, tiled=True)  110 us
    all_gather x1, waiting for transfers between devices, local(): lax.all_gather(low_qkv, 'dp', axis=0, tiled=True)  61 us
  transfers between devices with their start and end apart: 12, of which 11 were waited for; matrix products, arithmetic and copies ran while one was open for 8% of the time, Pallas kernels for 0%

commit v1 on v0

--- a/solution.py
+++ b/solution.py
@@ -1,3 +1,4 @@
+import functools
 import math
 import jax
 import jax.numpy as jnp
@@ -11,6 +12,39 @@
 RATE = 192.0
 KEEP = 0.9
 NEG = -1e30
+
+
+def sites_guide(incoming_x, chip_axis, join_dim):
+    f_next = lax.axis_index(chip_axis)
+    arr_next = lax.axis_size(chip_axis)
+    mat_out, extra, k_now = (arr_next, f_next, incoming_x.shape[join_dim])
+    taken_in = range(mat_out)
+    spare = map(lambda t: (t, (t + 1) % mat_out), taken_in)
+    p_next = range(mat_out)
+    line_up = list(spare)
+    e_now = map(lambda t: (t, (t - 1) % mat_out), p_next)
+    ledger = list(e_now)
+    part_next = jnp.zeros(
+        (*incoming_x.shape[:join_dim], mat_out * k_now, *incoming_x.shape[join_dim + 1 :]),
+        incoming_x.dtype,
+    )
+    wide_out = front = incoming_x
+    part_next = lax.dynamic_update_slice_in_dim(part_next, incoming_x, extra * k_now, axis=join_dim)
+    found_now = mat_out // 2
+    for dev in tuple(range(1, found_now + 1)):
+        wide_out = lax.ppermute(wide_out, chip_axis, line_up)
+        part_next = lax.dynamic_update_slice_in_dim(
+            part_next, wide_out, (extra - dev) % mat_out * k_now, axis=join_dim
+        )
+        if dev < mat_out - found_now:
+            front = lax.ppermute(front, chip_axis, ledger)
+            part_next = lax.dynamic_update_slice_in_dim(
+                part_next, front, (extra + dev) % mat_out * k_now, axis=join_dim
+            )
+    return part_next
+
+
+raise_threads = functools.partial(sites_guide, chip_axis="dp", join_dim=0)
 
 
 def layer_norm(value, gain, shift):
@@ -91,7 +125,7 @@
     w_qkv, w_proj, w_fc, w_down, w_norm = (
         lax.all_gather(low_qkv, "dp", axis=0, tiled=True),
         lax.all_gather(low_proj, "dp", axis=0, tiled=True),
-        lax.all_gather(low_fc, "dp", axis=0, tiled=True),
+        raise_threads(low_fc),
         lax.all_gather(low_down, "dp", axis=0, tiled=True),
         lax.all_gather(low_norm, "dp", axis=0, tiled=True),
     )

time: 2160 us -> 2040 us (0.944)
  waiting for transfers between devices: 1660 us -> 1480 us
  blocking collectives: 128 us -> 166 us
    psum x3, waiting for transfers between devices: 533 us -> 411 us  [sum_over_mp(): summed = lax.psum(term_fn(0, row_count), 'mp')]
    all_gather x1 -> x0, waiting for transfers between devices: 118 us -> none  [local(): lax.all_gather(low_fc, 'dp', axis=0, tiled=True)]
    ppermute x0 -> x7, waiting for transfers between devices: none -> 105 us  [the longest x4 61.5 us: sites_guide(): wide_out = lax.ppermute(wide_out, chip_axis, line_up)]
    all_gather x1, waiting for transfers between devices: 110 us -> 63.2 us  [local(): lax.all_gather(low_down, 'dp', axis=0, tiled=True)]
    psum x1, blocking collectives: 18.5 us -> 55.8 us  [local(): counts = lax.psum(local_counts, 'dp')]
  transfers between devices with their start and end apart: 12 -> 18, of which waited for: 11 -> 13; matrix products, arithmetic and copies ran while one was open for 8% -> 9% of each run, Pallas kernels for 0% -> 0%
where the time goes in v1:
time: 2040 us
  waiting for transfers between devices  1480 us (73%)
  matrix products  194 us (10%)
  blocking collectives  166 us (8%)
  other arithmetic  128 us (6%)
  local copies, waits for them, and re-layouts  34.5 us (2%)
  between operations  23.5 us (1%)
    psum x3, waiting for transfers between devices, sum_over_mp(): summed = lax.psum(term_fn(0, row_count), 'mp')  411 us
    reduce_scatter x1, waiting for transfers between devices, local(): lax.psum_scatter(fc_sum, 'dp', scatter_dimension=0, tiled=True)  282 us
    reduce_scatter x1, waiting for transfers between devices, local(): lax.psum_scatter(down_sum, 'dp', scatter_dimension=0, tiled=True)  282 us
    reduce_scatter x1, waiting for transfers between devices, local(): lax.psum_scatter(qkv_sum, 'dp', scatter_dimension=0, tiled=True)  208 us
    all_gather x1, waiting for transfers between devices, local(): lax.all_gather(low_down, 'dp', axis=0, tiled=True)  63.2 us
    ppermute x4, waiting for transfers between devices, sites_guide(): wide_out = lax.ppermute(wide_out, chip_axis, line_up)  61.5 us
    all_gather x1, waiting for transfers between devices, local(): lax.all_gather(low_qkv, 'dp', axis=0, tiled=True)  61 us
    psum x1, blocking collectives, local(): counts = lax.psum(local_counts, 'dp')  55.8 us
  transfers between devices with their start and end apart: 18, of which 13 were waited for; matrix products, arithmetic and copies ran while one was open for 9% of the time, Pallas kernels for 0%

profile of v1, /device:TPU:0, one launch (start us, length us, event | category | flops | bytes accessed | tf_op | source)
XLA Modules:
  0.0 2035.3 jit_solution(15516491576927316506)
XLA Ops:
  7.3 2.6 copy.64
  12.8 2.8 convert_reduce_fusion
  15.6 3.4 fusion.15
  19.1 32.9 %all_gather.12 = bf16[2048,6]{0,1:T(8,128)(2,1)S(1)} all-gather(bf16[256,6]{0,1:T(8,128)(2,1)S(1)} %convert_element_type.108), channel_id=1, replica_groups=mesh['dp'=8,'mp'=4] {'dp'}, dimensions={0}, use_global_device_ids=true | all-gather | bytes 27648 | tf_op jit(solution)/shard_map/all_gather | solution.py:130
  52.7 61.0 %all-gather.4.cloned.1.call-done = bf16[2048,3,512]{0,2,1:T(8,128)(2,1)} async-done(((bf16[256,3,512]{0,2,1:T(8,128)(2,1)}), bf16[2048,3,512]{0,2,1:T(8,128)(2,1)}) %all-gather.4.cloned.1.call-update) | async-done | bytes 6291472 | tf_op jit(solution)/shard_map/all_gather | solution.py:126
  113.7 11.1 add_convert_fusion.2
  124.9 3.3 fusion
  128.3 3.7 exponential_reduce_fusion
  134.0 6.5 convolution_convert_fusion.1
  140.4 23.5 %all-gather.6.cloned.1.call-done = bf16[2048,512]{1,0:T(8,128)(2,1)} async-done(((bf16[256,512]{1,0:T(8,128)(2,1)}), bf16[2048,512]{1,0:T(8,128)(2,1)}) %all-gather.6.cloned.1.call-update) | async-done | bytes 2097168 | tf_op jit(solution)/shard_map/all_gather | solution.py:127
  163.9 7.4 fusion.66
  171.4 2.7 convert_element_type.120
  174.2 4.3 broadcast_in_dim.107
  178.5 2.7 constant_dynamic-update-slice_fusion.7
  182.1 3.8 collective-permute-start.1
  185.9 40.0 %collective-permute-done = bf16[256,2048]{1,0:T(8,128)(2,1)S(1)} collective-permute-done((bf16[256,2048]{1,0:T(8,128)(2,1)S(1)}, bf16[256,2048]{1,0:T(8,128)(2,1)S(1)}, u32[]{:S(2)}, u32[]{:S(2)}) %collective-permute-start) | collective-permute-done | bytes 1048608 | tf_op jit(solution)/shard_map/ppermute | solution.py:35
  225.9 2.5 collective-permute-start.2
  229.0 2.5 collective-permute-start.3
  231.6 21.5 %collective-permute-done.2 = bf16[256,2048]{1,0:T(8,128)(2,1)} collective-permute-done((bf16[256,2048]{1,0:T(8,128)(2,1)S(1)}, bf16[256,2048]{1,0:T(8,128)(2,1)}, u32[]{:S(2)}, u32[]{:S(2)}) %collective-permute-start.2) | collective-permute-done | bytes 1048608 | tf_op jit(solution)/shard_map/ppermute | solution.py:35
  254.4 55.8 %psum.58 = f32[4]{0:T(128)S(1)} all-reduce(f32[4]{0:T(128)S(1)} %fusion.44), channel_id=1, replica_groups=mesh['dp'=8,'mp'=4] {'dp'}, use_global_device_ids=true, to_apply=%region_9.10 | all-reduce | flops 4 | bytes 32 | tf_op jit(solution)/shard_map/psum | solution.py:110
  314.4 2.3 constant_dynamic-update-slice_fusion.6
  319.6 2.3 constant_dynamic-update-slice_fusion.4
  321.9 2.3 constant_dynamic-update-slice_fusion.3
  324.2 2.3 constant_dynamic-update-slice_fusion.2
  326.5 42.6 %collective-permute-done.5 = bf16[256,2048]{1,0:T(8,128)(2,1)S(1)} collective-permute-done((bf16[256,2048]{1,0:T(8,128)(2,1)}, bf16[256,2048]{1,0:T(8,128)(2,1)S(1)}, u32[]{:S(2)}, u32[]{:S(2)}) %collective-permute-start.5) | collective-permute-done | bytes 1048608 | tf_op jit(solution)/shard_map/ppermute | solution.py:40
  371.2 5.8 fusion.62
  378.0 2.3 copy-done
  380.3 13.7 fusion.51
  393.9 63.2 %all-gather.8.cloned.1.call-done = bf16[2048,2048]{1,0:T(8,128)(2,1)} async-done(((bf16[256,2048]{1,0:T(8,128)(2,1)}), bf16[2048,2048]{1,0:T(8,128)(2,1)}) %all-gather.8.cloned.1.call-update) | async-done | bytes 8388624 | tf_op jit(solution)/shard_map/all_gather | solution.py:129
  457.1 20.4 %convert_reduce_fusion.1 = (f32[2048]{0:T(1024)}, bf16[1024,2048]{1,0:T(8,128)(2,1)S(1)}) fusion(bf16[2048,2048]{1,0:T(8,128)(2,1)} %all-gather.8.cloned.1.call-done, bf16[1024,2048]{1,0:T(8,128)(2,1)} %param.27, f32[1024]{0:T(1024)S(1)} %fusion.41, f32[1024,2048]{1,0:T(8,128)} %fusion.51, f32[2048]{0:T(1024)S(1)} %copy-done.50), kind=kOutput, calls=%fused_computation.34 | convolution fusion | flops 8652847104 | bytes 25186304 | tf_op jit(solution)/shard_map/td,df->tf/dot_general | solution.py:185
  479.5 13.2 fusion.67
  492.7 18.3 fusion.49
  511.0 132.9 %all-reduce.8.cloned.1.call-done = f32[1024,2048]{1,0:T(8,128)} async-done(((f32[1024,2048]{1,0:T(8,128)}), f32[1024,2048]{1,0:T(8,128)}) %all-reduce.8.cloned.1.call-update) | async-done | bytes 8388624 | tf_op jit(solution)/shard_map/psum | solution.py:104
  643.9 7.5 multiply_reduce_fusion.1
  652.1 5.0 fusion.61
  657.1 6.3 fusion.33
  663.5 9.7 convolution_convert_fusion
  673.1 12.6 multiply_reduce_fusion
  685.7 12.1 multiply_convert_fusion
  697.9 2.9 multiply_convert_fusion.2
  705.5 11.0 convolution_bitcast_fusion
  717.8 9.5 fusion.23
  727.3 278.3 %all-reduce.10.cloned.1.call-done = (f32[1024,2048]{1,0:T(8,128)}, f32[1024,2048]{1,0:T(8,128)}) async-done(((f32[1024,2048]{1,0:T(8,128)}, f32[1024,2048]{1,0:T(8,128)}), (f32[1024,2048]{1,0:T(8,128)}, f32[1024,2048]{1,0:T(8,128)})) %all-reduce.10.cloned.1.call-update) | async-done | bytes 16777232 | tf_op jit(solution)/shard_map/psum | solution.py:104
  1005.7 6.3 fusion.53
  1014.0 3.9 fusion.10
  1018.0 10.2 fusion.20
  1029.2 13.6 fusion.36
  1043.4 16.4 fusion.50
  1060.1 17.1 fusion.27
  1077.9 37.8 %all-reduce = (f32[2,512]{1,0:T(2,128)S(1)}, f32[2048]{0:T(1024)S(1)}) all-reduce(f32[2,512]{1,0:T(2,128)S(1)} %convert_reduce_fusion.2, f32[2048]{0:T(1024)S(1)} %copy-done.49), channel_id=1, replica_groups=mesh['dp'=8,'mp'=4] {'dp'}, use_global_device_ids=true, to_apply=%region_28.29 | all-reduce | flops 3072 | bytes 24576 | tf_op jit(solution)/shard_map/psum | solution.py:265
  1119.6 2.4 multiply_reduce_fusion.7
  1122.0 41.7 %reduce-scatter.6.cloned.1.call-done = f32[256,6]{0,1:T(8,128)} async-done(((f32[2048,6]{0,1:T(8,128)}), f32[256,6]{0,1:T(8,128)}) %reduce-scatter.6.cloned.1.call-update) | async-done | bytes 6160 | tf_op jit(solution)/shard_map/reduce_scatter | solution.py:263
  1166.3 208.2 %reduce-scatter.8.cloned.1.call-done = f32[256,3,512]{2,0,1:T(8,128)} async-done(((f32[2048,3,512]{2,0,1:T(8,128)}), f32[256,3,512]{2,0,1:T(8,128)}) %reduce-scatter.8.cloned.1.call-update) | async-done | bytes 1572880 | tf_op jit(solution)/shard_map/reduce_scatter | solution.py:259
  1374.5 3.1 multiply_reduce_fusion.6
  1378.9 281.6 %reduce-scatter.12.cloned.1.call-done = f32[256,2048]{1,0:T(8,128)} async-done(((f32[2048,2048]{1,0:T(8,128)}), f32[256,2048]{1,0:T(8,128)}) %reduce-scatter.12.cloned.1.call-update) | async-done | bytes 2097168 | tf_op jit(solution)/shard_map/reduce_scatter | solution.py:261
  1660.5 3.4 multiply_reduce_fusion.5
  1664.5 281.6 %reduce-scatter.14.cloned.1.call-done = f32[256,2048]{1,0:T(8,128)} async-done(((f32[2048,2048]{1,0:T(8,128)}), f32[256,2048]{1,0:T(8,128)}) %reduce-scatter.14.cloned.1.call-update) | async-done | bytes 2097168 | tf_op jit(solution)/shard_map/reduce_scatter | solution.py:262
  1946.1 3.4 multiply_reduce_fusion.4
  1950.3 10.2 add_convert_fusion
  1960.4 39.2 %psum.63 = f32[]{:T(128)} all-reduce(f32[]{:T(128)S(6)} %add.326), channel_id=1, replica_groups=mesh['dp'=8,'mp'=4] {'dp','mp'}, use_global_device_ids=true, to_apply=%region_41.42 | all-reduce | flops 1 | bytes 8 | tf_op jit(solution)/shard_map/psum | solution.py:283
  2005.4 3.2 fusion.57
  2008.7 2.2 multiply_add_fusion.8
  2010.9 5.9 fusion.58
  2018.5 5.1 fusion.54
  (193 shorter events, 45.2 us)
Async XLA Ops:
  7.2 11.8 copy-start.41
  7.2 106.5 %all-gather.4.cloned.1.call-start = ((), (), s32[]{:S(2)}) async-start(), calls=%async_computation.5 | async-start | bytes 7077888 | tf_op jit(solution)/shard_map/all_gather | solution.py:126
  9.9 154.0 %all-gather.6.cloned.1.call-start = ((), (), s32[]{:S(2)}) async-start(), calls=%async_computation.6 | async-start | bytes 2359296 | tf_op jit(solution)/shard_map/all_gather | solution.py:127
  11.7 359.5 %all-reduce.6.cloned.1.call-start = ((), (), s32[]{:S(2)}) async-start(), calls=%async_computation.7 | async-start | bytes 16777216 | tf_op jit(solution)/shard_map/psum | solution.py:104
  15.6 109.2 %copy-start.29 = (f32[1024]{0:T(1024)}, f32[1024]{0:T(1024)S(1)}, u32[]{:S(2)}) copy-start(f32[1024]{0:T(1024)S(1)} %broadcast_multiply_fusion.8) | copy-start | bytes 12292
  19.0 105.8 %copy-start.33 = (f32[1024]{0:T(1024)}, f32[1024]{0:T(1024)S(1)}, u32[]{:S(2)}) copy-start(f32[1024]{0:T(1024)S(1)} %fusion.15) | copy-start | bytes 12292
  19.1 105.8 %copy-start.31 = (f32[1024]{0:T(1024)}, f32[1024]{0:T(1024)S(1)}, u32[]{:S(2)}) copy-start(f32[1024]{0:T(1024)S(1)} %fusion.42) | copy-start | bytes 12292
  52.6 72.3 %copy-start.27 = (f32[2048,1]{0,1:T(1,128)}, f32[2048,1]{0,1:T(1,128)S(1)}, u32[]{:S(2)}) copy-start(f32[2048,1]{0,1:T(1,128)S(1)} %get-tuple-element.125) | copy-start | bytes 24580
  52.6 72.3 %copy-start.47 = (f32[2048,1]{0,1:T(1,128)}, f32[2048,1]{0,1:T(1,128)S(1)}, u32[]{:S(2)}) copy-start(f32[2048,1]{0,1:T(1,128)S(1)} %get-tuple-element.126) | copy-start | bytes 24580
  52.6 325.4 %copy-start.45 = (f32[2048,1]{0,1:T(1,128)}, f32[2048,1]{0,1:T(1,128)S(1)}, u32[]{:S(2)}) copy-start(f32[2048,1]{0,1:T(1,128)S(1)} %get-tuple-element.123) | copy-start | bytes 24580
  140.4 30.9 %copy-start.56 = (bf16[4,128,1024]{2,1,0:T(8,128)(2,1)}, bf16[4,128,1024]{2,1,0:T(8,128)(2,1)S(1)}, u32[]{:S(2)}) copy-start(bf16[4,128,1024]{2,1,0:T(8,128)(2,1)S(1)} %convolution_convert_fusion.1) | copy-start | bytes 3145732
  171.3 139.0 %copy-start.55 = (s32[4]{0:T(128)S(1)}, s32[4]{0:T(128)}, u32[]{:S(2)}) copy-start(s32[4]{0:T(128)} %param.30) | copy-start | bytes 52
  171.3 285.8 %all-gather.8.cloned.1.call-start = ((), (), s32[]{:S(2)}) async-start(), calls=%async_computation.8 | async-start | bytes 9437184 | tf_op jit(solution)/shard_map/all_gather | solution.py:129
  174.1 469.7 %all-reduce.8.cloned.1.call-start = ((), (), s32[]{:S(2)}) async-start(), calls=%async_computation.9 | async-start | bytes 16777216 | tf_op jit(solution)/shard_map/psum | solution.py:104
  181.2 44.7 %collective-permute-start = (bf16[256,2048]{1,0:T(8,128)(2,1)S(1)}, bf16[256,2048]{1,0:T(8,128)(2,1)S(1)}, u32[]{:S(2)}, u32[]{:S(2)}) collective-permute-start(bf16[256,2048]{1,0:T(8,128)(2,1)S(1)} %get-tuple-element.119), channel_id=1, source_target_pairs={{0,4},{4,8},{8,12},{12,16},{16,20},{20,24},{24,28},{28,0},{1,5},{5... | collective-permute-start | bytes 3145736 | tf_op jit(solution)/shard_map/ppermute | solution.py:35
  182.1 46.9 %collective-permute-start.1 = (bf16[256,2048]{1,0:T(8,128)(2,1)S(1)}, bf16[256,2048]{1,0:T(8,128)(2,1)S(1)}, u32[]{:S(2)}, u32[]{:S(2)}) collective-permute-start(bf16[256,2048]{1,0:T(8,128)(2,1)S(1)} %get-tuple-element.119), channel_id=1, source_target_pairs={{0,28},{4,0},{8,4},{12,8},{16,12},{20,16},{24,20},{28,24},{1,29},{... | collective-permute-start | bytes 3145736 | tf_op jit(solution)/shard_map/ppermute | solution.py:40
  225.9 27.1 %collective-permute-start.2 = (bf16[256,2048]{1,0:T(8,128)(2,1)S(1)}, bf16[256,2048]{1,0:T(8,128)(2,1)}, u32[]{:S(2)}, u32[]{:S(2)}) collective-permute-start(bf16[256,2048]{1,0:T(8,128)(2,1)S(1)} %collective-permute-done), channel_id=1, source_target_pairs={{0,4},{4,8},{8,12},{12,16},{16,20},{20,24},{24,28},{28,0},{1,5},{5... | collective-permute-start | bytes 3145736 | tf_op jit(solution)/shard_map/ppermute | solution.py:35
  229.0 85.1 %collective-permute-start.3 = (bf16[256,2048]{1,0:T(8,128)(2,1)S(1)}, bf16[256,2048]{1,0:T(8,128)(2,1)}, u32[]{:S(2)}, u32[]{:S(2)}) collective-permute-start(bf16[256,2048]{1,0:T(8,128)(2,1)S(1)} %collective-permute-done.1), channel_id=1, source_target_pairs={{0,28},{4,0},{8,4},{12,8},{16,12},{20,16},{24,20},{28,24},{1,29},{... | collective-permute-start | bytes 3145736 | tf_op jit(solution)/shard_map/ppermute | solution.py:40
  253.0 63.7 %collective-permute-start.4 = (bf16[256,2048]{1,0:T(8,128)(2,1)}, bf16[256,2048]{1,0:T(8,128)(2,1)}, u32[]{:S(2)}, u32[]{:S(2)}) collective-permute-start(bf16[256,2048]{1,0:T(8,128)(2,1)} %collective-permute-done.2), channel_id=1, source_target_pairs={{0,4},{4,8},{8,12},{12,16},{16,20},{20,24},{24,28},{28,0},{1,5},{5... | collective-permute-start | bytes 3145736 | tf_op jit(solution)/shard_map/ppermute | solution.py:35
  314.1 55.0 %collective-permute-start.5 = (bf16[256,2048]{1,0:T(8,128)(2,1)}, bf16[256,2048]{1,0:T(8,128)(2,1)S(1)}, u32[]{:S(2)}, u32[]{:S(2)}) collective-permute-start(bf16[256,2048]{1,0:T(8,128)(2,1)} %collective-permute-done.3), channel_id=1, source_target_pairs={{0,28},{4,0},{8,4},{12,8},{16,12},{20,16},{24,20},{28,24},{1,29},{... | collective-permute-start | bytes 3145736 | tf_op jit(solution)/shard_map/ppermute | solution.py:40
  316.7 53.5 %collective-permute-start.6 = (bf16[256,2048]{1,0:T(8,128)(2,1)}, bf16[256,2048]{1,0:T(8,128)(2,1)S(1)}, u32[]{:S(2)}, u32[]{:S(2)}) collective-permute-start(bf16[256,2048]{1,0:T(8,128)(2,1)} %collective-permute-done.4), channel_id=1, source_target_pairs={{0,4},{4,8},{8,12},{12,16},{16,20},{20,24},{24,28},{28,0},{1,5},{5... | collective-permute-start | bytes 3145736 | tf_op jit(solution)/shard_map/ppermute | solution.py:35
  380.3 76.8 %copy-start.50 = (f32[2048]{0:T(1024)S(1)}, f32[2048]{0:T(1024)}, u32[]{:S(2)}) copy-start(f32[2048]{0:T(1024)} %param.35) | copy-start | bytes 24580
  492.7 513.0 %all-reduce.10.cloned.1.call-start = ((), (), s32[]{:S(2)}) async-start(), calls=%async_computation.15 | async-start | bytes 33554432 | tf_op jit(solution)/shard_map/psum | solution.py:104
  643.9 8.2 copy-start.5
  657.1 6.4 copy-start.4
  663.5 9.7 copy-start.19
  716.6 289.2 %copy-start.28 = (f32[2048,1]{0,1:T(1,128)S(1)}, f32[2048,1]{0,1:T(1,128)}, u32[]{:S(2)}) copy-start(f32[2048,1]{0,1:T(1,128)} %copy-done.27) | copy-start | bytes 24580
  716.6 289.1 %copy-start.30 = (f32[1024]{0:T(1024)S(1)}, f32[1024]{0:T(1024)}, u32[]{:S(2)}) copy-start(f32[1024]{0:T(1024)} %copy-done.29) | copy-start | bytes 12292
  716.6 403.0 %reduce-scatter.10.cloned.1.call-start = ((), (), s32[]{:S(2)}) async-start(), calls=%async_computation.12 | async-start | bytes 4718592 | tf_op jit(solution)/shard_map/reduce_scatter | solution.py:260
  727.3 284.8 %copy-start.34 = (f32[1024]{0:T(1024)S(1)}, f32[1024]{0:T(1024)}, u32[]{:S(2)}) copy-start(f32[1024]{0:T(1024)} %copy-done.33) | copy-start | bytes 12292
  727.3 284.8 %copy-start.32 = (f32[1024]{0:T(1024)S(1)}, f32[1024]{0:T(1024)}, u32[]{:S(2)}) copy-start(f32[1024]{0:T(1024)} %copy-done.31) | copy-start | bytes 12292
  727.3 436.4 %reduce-scatter.6.cloned.1.call-start = ((), (), s32[]{:S(2)}) async-start(), calls=%async_computation.10 | async-start | bytes 73728 | tf_op jit(solution)/shard_map/reduce_scatter | solution.py:263
  1005.7 6.4 copy-start.1
  1005.7 8.3 copy-start.3
  1017.9 11.2 copy-start.17
  1018.0 11.2 copy-start.48
  1028.9 345.6 %reduce-scatter.8.cloned.1.call-start = ((), (), s32[]{:S(2)}) async-start(), calls=%async_computation.11 | async-start | bytes 14155776 | tf_op jit(solution)/shard_map/reduce_scatter | solution.py:259
  1042.8 617.7 %reduce-scatter.12.cloned.1.call-start = ((), (), s32[]{:S(2)}) async-start(), calls=%async_computation.13 | async-start | bytes 18874368 | tf_op jit(solution)/shard_map/reduce_scatter | solution.py:261
  1059.9 886.2 %reduce-scatter.14.cloned.1.call-start = ((), (), s32[]{:S(2)}) async-start(), calls=%async_computation.14 | async-start | bytes 18874368 | tf_op jit(solution)/shard_map/reduce_scatter | solution.py:262
  1077.2 872.9 %copy-start.35 = (f32[2048,1]{0,1:T(1,128)S(1)}, f32[2048,1]{0,1:T(1,128)}, u32[]{:S(2)}) copy-start(f32[2048,1]{0,1:T(1,128)} %get-tuple-element.121) | copy-start | bytes 24580
  1950.1 50.2 %copy-start.51 = (f32[2048]{0:T(1024)S(1)}, f32[2048]{0:T(1024)}, u32[]{:S(2)}) copy-start(f32[2048]{0:T(1024)} %param.42) | copy-start | bytes 24580
  1950.1 51.6 %copy-start.42 = (f32[2,512]{1,0:T(2,128)S(1)}, f32[2,512]{1,0:T(2,128)}, u32[]{:S(2)}) copy-start(f32[2,512]{1,0:T(2,128)} %param.32) | copy-start | bytes 12292
  1950.2 51.6 %copy-start.54 = (f32[2,512]{1,0:T(2,128)S(1)}, f32[2,512]{1,0:T(2,128)}, u32[]{:S(2)}) copy-start(f32[2,512]{1,0:T(2,128)} %param.39) | copy-start | bytes 12292
  1950.2 52.2 %copy-start.53 = (f32[2,512]{1,0:T(2,128)S(1)}, f32[2,512]{1,0:T(2,128)}, u32[]{:S(2)}) copy-start(f32[2,512]{1,0:T(2,128)} %param.46) | copy-start | bytes 12292
  1950.2 52.7 %copy-start.43 = (f32[2048]{0:T(1024)S(1)}, f32[2048]{0:T(1024)}, u32[]{:S(2)}) copy-start(f32[2048]{0:T(1024)} %param.49) | copy-start | bytes 24580
  1950.2 53.3 %copy-start.38 = (f32[256,6]{0,1:T(8,128)S(1)}, f32[256,6]{0,1:T(8,128)}, u32[]{:S(2)}) copy-start(f32[256,6]{0,1:T(8,128)} %param.31) | copy-start | bytes 18436
  1950.2 53.3 %copy-start.39 = (f32[256,6]{0,1:T(8,128)S(1)}, f32[256,6]{0,1:T(8,128)}, u32[]{:S(2)}) copy-start(f32[256,6]{0,1:T(8,128)} %reduce-scatter.6.cloned.1.call-done) | copy-start | bytes 18436
  1950.2 53.3 %copy-start.52 = (f32[256,6]{0,1:T(8,128)S(1)}, f32[256,6]{0,1:T(8,128)}, u32[]{:S(2)}) copy-start(f32[256,6]{0,1:T(8,128)} %param.38) | copy-start | bytes 18436
  1950.2 54.6 %copy-start.44 = (f32[256,6]{0,1:T(8,128)S(1)}, f32[256,6]{0,1:T(8,128)}, u32[]{:S(2)}) copy-start(f32[256,6]{0,1:T(8,128)} %param.45) | copy-start | bytes 18436
  1950.2 60.6 %copy-start.12 = (f32[256,3,512]{2,0,1:T(8,128)S(1)}, f32[256,3,512]{2,0,1:T(8,128)}, u32[]{:S(2)}) copy-start(f32[256,3,512]{2,0,1:T(8,128)} %param.33) | copy-start | bytes 4718596
  1950.3 60.6 %copy-start.13 = (f32[256,3,512]{2,0,1:T(8,128)S(1)}, f32[256,3,512]{2,0,1:T(8,128)}, u32[]{:S(2)}) copy-start(f32[256,3,512]{2,0,1:T(8,128)} %reduce-scatter.8.cloned.1.call-done) | copy-start | bytes 4718596
  2000.3 16.5 copy-start.25
  2001.7 16.7 copy-start.36
  2002.3 16.1 copy-start.40
  2004.8 13.7 copy-start.37
  2008.6 15.0 copy-start.22
  2008.7 9.8 copy-start.8
  2008.7 9.8 copy-start.9
  2008.7 9.8 copy-start.10
  2008.7 9.8 copy-start.11
  2008.7 9.8 copy-start.23
  2008.7 9.8 copy-start.24
  2016.8 6.9 copy-start.14
  2018.5 7.2 copy-start.21
  (13 other events, 43.6 us)
Sparse Core Ops, SparseCore 0:
  10.7 102.9 all-gather.3
  116.4 47.4 all-gather.5
  171.4 151.3 all-reduce.5
  325.4 131.6 all-gather.7
  492.8 151.0 all-reduce.7
  716.7 288.9 all-reduce.9
  1009.9 88.2 reduce-scatter.9
  1102.5 61.1 reduce-scatter.5
  1167.8 206.6 reduce-scatter.7
  1378.6 281.8 reduce-scatter.11
  1664.3 281.7 reduce-scatter.13
